TPU v7x, 512 devices: a whole 4x4x16 slice. The times are simulated.
512 devices in a mesh: wide: 64 (over z, x), narrow: 8 (over y, core).
Axes of the slice: x: 4, y: 4, z: 16, core: 2. Of those that a mesh axis runs over, the one named last changes fastest.
Arguments:
- tokens: bfloat16 [128, 8192], P('wide', 'narrow'), may hold values from -6 to 6
- cotangent: bfloat16 [128, 8192], P('wide', 'narrow'), may hold values from -6 to 6
- gate_tiles: bfloat16 [8, 64, 12, 128, 128], P('narrow', 'wide'), may hold values from -0.109375 to 0.109375
- up_tiles: bfloat16 [8, 64, 12, 128, 128], P('narrow', 'wide'), may hold values from -0.109375 to 0.109375
- down_tiles: bfloat16 [8, 64, 12, 128, 128], P('narrow', 'wide'), may hold values from -0.0625 to 0.0625
- kept_slots: int32 [3, 8, 64, 12], P(None, 'narrow', 'wide'), may hold values from 0 to 23, as said below
- kept_counts: int32 [3, 8, 64], P(None, 'narrow', 'wide'), may hold values from 3 to 12, as said below
Outputs:
- layer_out: bfloat16 [128, 8192], P('wide', 'narrow')
- input_grad: bfloat16 [128, 8192], P('wide', 'narrow')
- gate_grad: bfloat16 [8, 64, 12, 128, 128], P('narrow', 'wide')
- up_grad: bfloat16 [8, 64, 12, 128, 128], P('narrow', 'wide')
- down_grad: bfloat16 [8, 64, 12, 128, 128], P('narrow', 'wide')
Inputs may be any that keep to these rules, and one draw needn't show every extreme that they name: `kept_slots`: for each matrix and device the first 12 entries are distinct local tile positions. `kept_counts`: for each matrix some device keeps exactly 12 tiles.
All inputs are finite; a program needn't handle non-finite values.
Results may differ from a plain program's by a relative error of at most 0.005.
Values may be sent and summed in bfloat16 or wider, within the bound.
A program may use at most 64 MiB of HBM per device.

v0:
```python
import jax
import jax.numpy as jnp
from jax import lax
from jax.sharding import PartitionSpec as P

HT_DEV = 3


highest = lax.Precision.HIGHEST


def from_everyone(shard, axis):
    copies = jnp.broadcast_to(shard, (lax.axis_size(axis), *shard.shape))
    return lax.all_to_all(copies, axis, split_axis=0, concat_axis=0, tiled=True)


def joined_along(pieces, dim):
    pieces = jnp.moveaxis(pieces, 0, dim)
    shape = pieces.shape
    return pieces.reshape(*shape[:dim], shape[dim] * shape[dim + 1], *shape[dim + 2 :])


def gather_directly(shard, axis, dim):
    pieces = from_everyone(shard, axis)
    return joined_along(pieces, dim)


def side_by_side(arrays, axis, dim, along):
    ends, at = ([], 0)
    for a in arrays[:-1]:
        at += a.shape[along]
        ends.append(at)
    both = jnp.concatenate(arrays, axis=along)
    return tuple(
        jnp.split(lax.psum_scatter(both, axis, scatter_dimension=dim, tiled=True), ends, axis=along)
    )


def split_up(shard, dim, count):
    before, after = (shard.shape[:dim], shard.shape[dim + 1 :])
    return jnp.moveaxis(shard.reshape(*before, count, -1, *after), dim, 0)


def sent_and_summed(shard, axis, dim):
    count = lax.axis_size(axis)
    pieces = lax.all_to_all(split_up(shard, dim, count), axis, 0, 0, tiled=True)
    return jnp.sum(pieces, axis=0)


def side_by_side_2(arrays, axis, dim, along):
    both = jnp.concatenate(arrays, axis=along)
    result, at, finished = (lax.all_gather(both, axis, axis=dim, tiled=True), 0, [])
    for a in arrays:
        finished.append(lax.slice_in_dim(result, at, at + a.shape[along], axis=along))
        at += a.shape[along]
    return tuple(finished)


def onehots(slot_list, kept_count, row_tiles, col_tiles):
    row_onehot = (
        slot_list[:, None] // col_tiles == jnp.arange(row_tiles, dtype=jnp.int32)[None, :]
    ).astype(jnp.float32)
    col_onehot = (
        slot_list[:, None] % col_tiles == jnp.arange(col_tiles, dtype=jnp.int32)[None, :]
    ).astype(jnp.float32)
    live_mask = (jnp.arange(slot_list.shape[0], dtype=jnp.int32) < kept_count).astype(jnp.float32)
    return (row_onehot, col_onehot, live_mask)


def tile_product(panel_in, tiles, slot_list, kept_count, col_tiles):
    row_onehot, col_onehot, live_mask = onehots(slot_list, kept_count, panel_in.shape[1], col_tiles)
    picked = jnp.einsum(
        "tra,kr->kta",
        panel_in,
        row_onehot.astype(jnp.bfloat16),
        preferred_element_type=jnp.bfloat16,
    )
    product = jnp.einsum("kta,kab->ktb", picked, tiles, preferred_element_type=jnp.float32)
    return jnp.einsum(
        "ktb,kc->tcb",
        product,
        col_onehot * live_mask[:, None],
        precision=highest,
        preferred_element_type=jnp.float32,
    )


def tile_transposed(panel_out, tiles, slot_list, kept_count, row_tiles):
    row_onehot, col_onehot, live_mask = onehots(
        slot_list, kept_count, row_tiles, panel_out.shape[1]
    )
    picked = jnp.einsum(
        "tcb,kc->ktb",
        panel_out,
        col_onehot.astype(jnp.bfloat16),
        preferred_element_type=jnp.bfloat16,
    )
    product = jnp.einsum("ktb,kab->kta", picked, tiles, preferred_element_type=jnp.float32)
    return jnp.einsum(
        "kta,kr->tra",
        product,
        row_onehot * live_mask[:, None],
        precision=highest,
        preferred_element_type=jnp.float32,
    )


def tile_grad(panel_in, panel_out, slot_list, kept_count):
    row_onehot, col_onehot, live_mask = onehots(
        slot_list, kept_count, panel_in.shape[1], panel_out.shape[1]
    )
    picked_in = jnp.einsum(
        "tra,kr->kta",
        panel_in,
        row_onehot.astype(jnp.bfloat16),
        preferred_element_type=jnp.bfloat16,
    )
    picked_out = jnp.einsum(
        "tcb,kc->ktb",
        panel_out,
        col_onehot.astype(jnp.bfloat16),
        preferred_element_type=jnp.bfloat16,
    )
    grads = jnp.einsum("kta,ktb->kab", picked_in, picked_out, preferred_element_type=jnp.float32)
    return (grads * live_mask[:, None, None]).astype(jnp.bfloat16)


def activate(gate_sum, up_sum):
    return (jax.nn.silu(gate_sum) * up_sum).astype(jnp.bfloat16)


def gate_grads(hidden_grad, gate_sum, up_sum):
    sigmoid_gate = jax.nn.sigmoid(gate_sum)
    gate_act = (
        hidden_grad * up_sum * sigmoid_gate * (1.0 + gate_sum * (1.0 - sigmoid_gate))
    ).astype(jnp.bfloat16)
    up_act = (hidden_grad * gate_sum * sigmoid_gate).astype(jnp.bfloat16)
    return (gate_act, up_act)


def per_device(tokens, cotangent, gate_tiles, up_tiles, down_tiles, kept_slots, kept_counts):
    tile_size = gate_tiles.shape[-1]
    row_blocks = tokens.shape[1] // tile_size
    own_rows = tokens.shape[0]
    gate_slots, up_slots, down_slots = (
        kept_slots[0, 0, 0],
        kept_slots[1, 0, 0],
        kept_slots[2, 0, 0],
    )
    gate_count, up_count, down_count = (
        kept_counts[0, 0, 0],
        kept_counts[1, 0, 0],
        kept_counts[2, 0, 0],
    )
    gate_block, up_block, down_block = (gate_tiles[0, 0], up_tiles[0, 0], down_tiles[0, 0])
    token_panel = gather_directly(tokens, "wide", 0)
    row_count = token_panel.shape[0]
    token_panel3 = token_panel.reshape(row_count, row_blocks, tile_size)
    gate_part = tile_product(token_panel3, gate_block, gate_slots, gate_count, HT_DEV).reshape(
        row_count, -1
    )
    up_part = tile_product(token_panel3, up_block, up_slots, up_count, HT_DEV).reshape(
        row_count, -1
    )
    gate_sum, up_sum = side_by_side((gate_part, up_part), "narrow", 0, 1)
    hidden = gather_directly(activate(gate_sum, up_sum), "narrow", 0)
    hidden3 = hidden.reshape(row_count, HT_DEV, tile_size)
    layer_out = sent_and_summed(
        tile_product(hidden3, down_block, down_slots, down_count, row_blocks).reshape(
            own_rows * lax.axis_size("wide"), -1
        ),
        "wide",
        0,
    ).astype(jnp.bfloat16)
    grad_panel = gather_directly(cotangent, "wide", 0)
    grad_panel3 = grad_panel.reshape(row_count, row_blocks, tile_size)
    hidden_part = tile_transposed(grad_panel3, down_block, down_slots, down_count, HT_DEV).reshape(
        row_count, -1
    )
    hidden_grad = sent_and_summed(hidden_part, "narrow", 0)
    gate_share, up_share = gate_grads(hidden_grad, gate_sum, up_sum)
    gate_act, up_act = side_by_side_2((gate_share, up_share), "narrow", 0, 1)
    gate_act3 = gate_act.reshape(row_count, HT_DEV, tile_size)
    up_act3 = up_act.reshape(row_count, HT_DEV, tile_size)
    down_grad = tile_grad(hidden3, grad_panel3, down_slots, down_count)[None, None]
    gate_grad = tile_grad(token_panel3, gate_act3, gate_slots, gate_count)[None, None]
    up_grad = tile_grad(token_panel3, up_act3, up_slots, up_count)[None, None]
    first = tile_transposed(gate_act3, gate_block, gate_slots, gate_count, row_blocks)
    second = tile_transposed(up_act3, up_block, up_slots, up_count, row_blocks)
    input_grad = sent_and_summed(
        (first + second).reshape(own_rows * lax.axis_size("wide"), -1), "wide", 0
    ).astype(jnp.bfloat16)
    return (layer_out, input_grad, gate_grad, up_grad, down_grad)


def solution(mesh):
    in_specs = (
        P("wide", "narrow"),
        P("wide", "narrow"),
        P("narrow", "wide", None, None, None),
        P("narrow", "wide", None, None, None),
        P("narrow", "wide", None, None, None),
        P(None, "narrow", "wide", None),
        P(None, "narrow", "wide"),
    )
    out_specs = (
        P("wide", "narrow"),
        P("wide", "narrow"),
        P("narrow", "wide", None, None, None),
        P("narrow", "wide", None, None, None),
        P("narrow", "wide", None, None, None),
    )
    return jax.shard_map(
        per_device, mesh=mesh, in_specs=in_specs, out_specs=out_specs, check_vma=False
    )
```

profile of v0, /device:TPU:24, one launch (start us, length us, event | category | flops | bytes accessed | tf_op | source)
XLA Modules:
  0.0 221.5 jit_solution(11882330474304203076)
XLA Ops:
  7.2 1.6 broadcast_in_dim.12
  8.8 18.7 %all-to-all-start = ((bf16[64,2,1024]{2,1,0:T(2,128)(2,1)}), bf16[64,2,1024]{2,1,0:T(2,128)(2,1)S(1)}, u32[]{:S(2)}, u32[]{:S(2)}) async-start(bf16[64,2,1024]{2,1,0:T(2,128)(2,1)} %broadcast_in_dim.12), calls=%async_computation | async-start | bytes 524288 | tf_op jit(solution)/shard_map/all_to_all | solution.py:14
  30.1 19.8 %all-to-all-done = bf16[64,2,1024]{2,1,0:T(2,128)(2,1)S(1)} async-done(((bf16[64,2,1024]{2,1,0:T(2,128)(2,1)}), bf16[64,2,1024]{2,1,0:T(2,128)(2,1)S(1)}, u32[]{:S(2)}, u32[]{:S(2)}) %all-to-all-start) | async-done | bytes 262176 | tf_op jit(solution)/shard_map/all_to_all | solution.py:14
  50.7 5.0 %all-to-all-start.3 = ((bf16[64,2,1024]{2,1,0:T(2,128)(2,1)}), bf16[64,2,1024]{2,1,0:T(2,128)(2,1)S(1)}, u32[]{:S(2)}, u32[]{:S(2)}) async-start(bf16[64,2,1024]{2,1,0:T(2,128)(2,1)} %broadcast_in_dim.14), calls=%async_computation.3 | async-start | bytes 524288 | tf_op jit(solution)/shard_map/all_to_all | solution.py:14
  57.8 1.1 convolution_bitcast_fusion.3
  60.2 1.1 convolution_bitcast_fusion.2
  62.3 15.2 %all-to-all-done.3 = bf16[64,2,1024]{2,1,0:T(2,128)(2,1)S(1)} async-done(((bf16[64,2,1024]{2,1,0:T(2,128)(2,1)}), bf16[64,2,1024]{2,1,0:T(2,128)(2,1)S(1)}, u32[]{:S(2)}, u32[]{:S(2)}) %all-to-all-start.3) | async-done | bytes 262176 | tf_op jit(solution)/shard_map/all_to_all | solution.py:14
  79.1 1.1 convolution_bitcast_fusion.1
  80.3 9.5 %all_to_all.30 = f32[8,16,384]{2,1,0:T(8,128)S(1)} all-to-all(f32[8,16,384]{2,1,0:T(8,128)S(1)} %reshape_reshape.22), channel_id=1, replica_groups=mesh['wide'=64,'narrow'=8] {'narrow'}, dimensions={0} | all-to-all | bytes 393216 | tf_op jit(solution)/shard_map/all_to_all | solution.py:46
  89.8 9.6 %reduce-scatter.4.cloned.1.call-done = f32[16,768]{1,0:T(8,128)} async-done(((f32[128,768]{1,0:T(8,128)}), f32[16,768]{1,0:T(8,128)}) %reduce-scatter.4.cloned.1.call-update) | async-done | bytes 49168 | tf_op jit(solution)/shard_map/reduce_scatter | solution.py:35
  100.8 6.8 %all-to-all-start.1 = ((bf16[8,16,384]{2,1,0:T(8,128)(2,1)}), bf16[8,16,384]{2,1,0:T(8,128)(2,1)S(1)}, u32[]{:S(2)}, u32[]{:S(2)}) async-start(bf16[8,16,384]{2,1,0:T(8,128)(2,1)} %broadcast_in_dim.13), calls=%async_computation.1 | async-start | bytes 196608 | tf_op jit(solution)/shard_map/all_to_all | solution.py:14
  107.6 13.0 %all_gather.3 = bf16[128,768]{1,0:T(8,128)(2,1)S(1)} all-gather(bf16[16,768]{1,0:T(8,128)(2,1)S(1)} %pad_maximum_fusion.1), channel_id=1, replica_groups=mesh['wide'=64,'narrow'=8] {'narrow'}, dimensions={0}, use_global_device_ids=true | all-gather | bytes 221184 | tf_op jit(solution)/shard_map/all_gather | solution.py:52
  121.9 1.1 fusion.8
  123.7 1.1 fusion.3
  125.8 15.5 %all-to-all-start.5 = ((f32[64,2,1024]{2,1,0:T(2,128)}), f32[64,2,1024]{2,1,0:T(2,128)}, u32[]{:S(2)}, u32[]{:S(2)}) async-start(f32[64,2,1024]{2,1,0:T(2,128)} %reshape_reshape.23), calls=%async_computation.5 | async-start | bytes 1048576 | tf_op jit(solution)/shard_map/all_to_all | solution.py:46
  141.4 1.2 fusion.68
  142.6 1.4 copy.53
  144.3 1.9 convolution_bitcast_fusion
  146.2 2.1 reshape_reshape.20
  148.4 26.2 %all-to-all-done.5 = f32[64,2,1024]{2,1,0:T(2,128)} async-done(((f32[64,2,1024]{2,1,0:T(2,128)}), f32[64,2,1024]{2,1,0:T(2,128)}, u32[]{:S(2)}, u32[]{:S(2)}) %all-to-all-start.5) | async-done | bytes 524320 | tf_op jit(solution)/shard_map/all_to_all | solution.py:46
  174.5 6.1 %all-to-all-start.2 = ((f32[64,2,1024]{2,1,0:T(2,128)}), f32[64,2,1024]{2,1,0:T(2,128)}, u32[]{:S(2)}, u32[]{:S(2)}) async-start(f32[64,2,1024]{2,1,0:T(2,128)} %reshape_reshape.20), calls=%async_computation.2 | async-start | bytes 1048576 | tf_op jit(solution)/shard_map/all_to_all | solution.py:46
  183.7 1.8 reduce_sum.29
  185.5 27.4 %all-to-all-done.2 = f32[64,2,1024]{2,1,0:T(2,128)} async-done(((f32[64,2,1024]{2,1,0:T(2,128)}), f32[64,2,1024]{2,1,0:T(2,128)}, u32[]{:S(2)}, u32[]{:S(2)}) %all-to-all-start.2) | async-done | bytes 524320 | tf_op jit(solution)/shard_map/all_to_all | solution.py:46
  212.8 1.8 reduce_sum.27
  (58 shorter events, 17.3 us)
Async XLA Ops:
  7.2 49.5 %copy-start = (bf16[1,1,12,128,128]{4,3,2,1,0:T(8,128)(2,1)S(1)}, bf16[1,1,12,128,128]{4,3,2,1,0:T(8,128)(2,1)}, u32[]{:S(2)}) copy-start(bf16[1,1,12,128,128]{4,3,2,1,0:T(8,128)(2,1)} %param.9) | copy-start | bytes 1179652
  8.8 18.7 %copy-start.4 = (s32[3,1,1]{0,2,1:T(1,128)S(1)}, s32[3,1,1]{0,2,1:T(1,128)}, u32[]{:S(2)}) copy-start(s32[3,1,1]{0,2,1:T(1,128)} %param.13) | copy-start | bytes 40
  8.8 41.1 %all-to-all-start = ((bf16[64,2,1024]{2,1,0:T(2,128)(2,1)}), bf16[64,2,1024]{2,1,0:T(2,128)(2,1)S(1)}, u32[]{:S(2)}, u32[]{:S(2)}) async-start(bf16[64,2,1024]{2,1,0:T(2,128)(2,1)} %broadcast_in_dim.12), calls=%async_computation | async-start | bytes 524288 | tf_op jit(solution)/shard_map/all_to_all | solution.py:14
  29.4 0.7 copy-start.6
  30.1 19.8 %copy-start.5 = (bf16[2,1024]{1,0:T(2,128)(2,1)S(1)}, bf16[2,1024]{1,0:T(2,128)(2,1)}, u32[]{:S(2)}) copy-start(bf16[2,1024]{1,0:T(2,128)(2,1)} %param.8) | copy-start | bytes 12292
  50.7 26.8 %all-to-all-start.3 = ((bf16[64,2,1024]{2,1,0:T(2,128)(2,1)}), bf16[64,2,1024]{2,1,0:T(2,128)(2,1)S(1)}, u32[]{:S(2)}, u32[]{:S(2)}) async-start(bf16[64,2,1024]{2,1,0:T(2,128)(2,1)} %broadcast_in_dim.14), calls=%async_computation.3 | async-start | bytes 524288 | tf_op jit(solution)/shard_map/all_to_all | solution.py:14
  55.7 43.7 %reduce-scatter.4.cloned.1.call-start = ((), (), s32[]{:S(2)}) async-start(), calls=%async_computation.7 | async-start | bytes 442368 | tf_op jit(solution)/shard_map/reduce_scatter | solution.py:35
  58.8 1.0 copy-start.1
  77.7 1.0 copy-start.2
  100.8 25.0 %all-to-all-start.1 = ((bf16[8,16,384]{2,1,0:T(8,128)(2,1)}), bf16[8,16,384]{2,1,0:T(8,128)(2,1)S(1)}, u32[]{:S(2)}, u32[]{:S(2)}) async-start(bf16[8,16,384]{2,1,0:T(8,128)(2,1)} %broadcast_in_dim.13), calls=%async_computation.1 | async-start | bytes 196608 | tf_op jit(solution)/shard_map/all_to_all | solution.py:14
  125.8 48.7 %all-to-all-start.5 = ((f32[64,2,1024]{2,1,0:T(2,128)}), f32[64,2,1024]{2,1,0:T(2,128)}, u32[]{:S(2)}, u32[]{:S(2)}) async-start(f32[64,2,1024]{2,1,0:T(2,128)} %reshape_reshape.23), calls=%async_computation.5 | async-start | bytes 1048576 | tf_op jit(solution)/shard_map/all_to_all | solution.py:46
  142.6 1.4 copy-start.3
  174.5 38.3 %all-to-all-start.2 = ((f32[64,2,1024]{2,1,0:T(2,128)}), f32[64,2,1024]{2,1,0:T(2,128)}, u32[]{:S(2)}, u32[]{:S(2)}) async-start(f32[64,2,1024]{2,1,0:T(2,128)} %reshape_reshape.20), calls=%async_computation.2 | async-start | bytes 1048576 | tf_op jit(solution)/shard_map/all_to_all | solution.py:46
Sparse Core Ops, SparseCore 0:
  62.5 36.8 reduce-scatter.3
where the time goes:
time: 223 us; the launch traced here: 222 us
  waiting for transfers between devices  98.1 us (44%)
  starting transfers between devices  52.1 us (23%)
  blocking collectives  22.4 us (10%)
  matrix products  15.3 us (7%)
  between operations  14.4 us (6%)
  local copies, waits for them, and re-layouts  12.8 us (6%)
  other arithmetic  6.43 us (3%)
    all_to_all x2, waiting for transfers between devices, sent_and_summed(): pieces = lax.all_to_all(split_up(shard, dim, count), axis, 0, 0, tiled=True)  53.5 us
    all_to_all x3, waiting for transfers between devices, from_everyone(): return lax.all_to_all(copies, axis, split_axis=0, concat_axis=0, tiled=True)  35 us
    all_to_all x3, starting transfers between devices, from_everyone(): return lax.all_to_all(copies, axis, split_axis=0, concat_axis=0, tiled=True)  30.4 us
    all_to_all x2, starting transfers between devices, sent_and_summed(): pieces = lax.all_to_all(split_up(shard, dim, count), axis, 0, 0, tiled=True)  21.6 us
    all_gather x1, blocking collectives, side_by_side_2(): lax.all_gather(both, axis, axis=dim, tiled=True)  13 us
    reduce_scatter x1, waiting for transfers between devices, side_by_side(): lax.psum_scatter(both, axis, scatter_dimension=dim, tiled=True)  9.61 us
    all_to_all x1, blocking collectives, sent_and_summed(): pieces = lax.all_to_all(split_up(shard, dim, count), axis, 0, 0, tiled=True)  9.49 us
  transfers between devices with their start and end apart: 6, of which 5 were waited for; matrix products, arithmetic and copies ran while one was open for 12% of the time, Pallas kernels for 0%

commit v1 on v0

v1 whole, which is shorter than its diff:
```python
import functools

import jax
import jax.numpy as jnp
from jax import lax
from jax.experimental import pallas as pl
from jax.experimental.pallas import tpu as pltpu
from jax.sharding import PartitionSpec as P

TILE = 128
HT = 3
DT = 8
LOC = HT * DT
X_SIZE = 4
REACH = 2
F32, BF16 = jnp.float32, jnp.bfloat16
MESH = pl.DeviceIdType.MESH


def layer_kernel(
    nz, nx, nn, cap,
    slots, counts, tok_hbm, cot_hbm, gate_hbm, up_hbm, down_hbm,
    layer_out, input_grad, gate_grad, up_grad, down_grad,
    own_in, pair, gathered, tiles, w_in, w_down, rows, tok, cot, tok_t, hid_t, act,
    part, part_in, acts, back, back_in, back_sum, last_in, grads,
    sem_in, sem_out, zs, zr, xs, xr, ps, pr, as_, ar, bs, br, ls, lr,
):
    wide, me = lax.axis_index("wide"), lax.axis_index("narrow")
    z, x = wide // nx, wide % nx
    half = nz // 2
    width = HT * TILE
    tokens = 2 * nz * nx
    own_rows = tokens // nn
    per_z = 2 * nx

    def at_z(step):
        return ((z + step + nz) % nz * nx + x, me)

    def at_x(step):
        return (z * nx + (x + step) % nx, me)

    def at_n(step):
        return (wide, (me + step) % nn)

    def remote(src, dst, send, recv, target):
        return pltpu.make_async_remote_copy(
            src_ref=src, dst_ref=dst, send_sem=send, recv_sem=recv,
            device_id=target, device_id_type=MESH,
        )

    loads = [
        pltpu.make_async_copy(tok_hbm, own_in.at[0], sem_in.at[0]),
        pltpu.make_async_copy(cot_hbm, own_in.at[1], sem_in.at[1]),
        pltpu.make_async_copy(gate_hbm, tiles.at[0], sem_in.at[2]),
        pltpu.make_async_copy(up_hbm, tiles.at[1], sem_in.at[3]),
        pltpu.make_async_copy(down_hbm, tiles.at[2], sem_in.at[4]),
    ]
    for load in loads:
        load.start()

    barrier = pltpu.get_barrier_semaphore()
    z_near = sorted({s % nz for d in range(1, REACH + 1) for s in (d, -d)})
    for step in z_near:
        pl.semaphore_signal(barrier, inc=1, device_id=at_z(step), device_id_type=MESH)
    for step in range(1, nx):
        pl.semaphore_signal(barrier, inc=1, device_id=at_x(step), device_id_type=MESH)
    for step in range(1, nn):
        pl.semaphore_signal(barrier, inc=1, device_id=at_n(step), device_id_type=MESH)

    loads[0].wait()
    loads[1].wait()
    for o in range(2):
        both = own_in[o].astype(F32)
        for k in range(DT):
            for i in range(2):
                pair[o, pl.ds(8 * i + k, 1), :] = both[i : i + 1, k * TILE : (k + 1) * TILE]
        gathered[x, 0, o] = pair[o].astype(BF16)

    pl.semaphore_wait(barrier, len(z_near) + nx - 1 + nn - 1)

    def z_copy(slot, to_slot, step):
        return remote(
            gathered.at[x, slot], gathered.at[x, to_slot],
            zs.at[to_slot], zr.at[to_slot], at_z(step),
        )

    def x_copy(slot, step):
        return remote(
            gathered.at[x, slot], gathered.at[x, slot],
            xs.at[step - 1, slot], xr.at[step - 1, slot], at_x(step),
        )

    for d in range(1, REACH + 1):
        z_copy(0, nz - d, d).start()
        if d < half:
            z_copy(0, d, -d).start()
    for step in range(1, nx):
        x_copy(0, step).start()

    def relay(d, carry):
        up = nz - d
        z_copy(up, up, 0).wait_recv()

        @pl.when(d + REACH <= half)
        def _():
            z_copy(up, up - REACH, REACH).start()

        for step in range(1, nx):
            x_copy(up, step).start()

        @pl.when(d < half)
        def _():
            z_copy(d, d, 0).wait_recv()

            @pl.when(d + REACH < half)
            def _():
                z_copy(d, d + REACH, -REACH).start()

            for step in range(1, nx):
                x_copy(d, step).start()

        return carry

    for load in loads[2:]:
        load.wait()

    def place(p, carry):
        for m in range(3):
            found, live = jnp.int32(0), jnp.int32(0)
            for s in range(cap):
                hit = jnp.logical_and(slots[m, 0, 0, s] == p, s < counts[m, 0, 0])
                found = jnp.where(hit, s, found)
                live = jnp.where(hit, 1, live)
            tile = (tiles[m, found].astype(F32) * live.astype(F32)).astype(BF16)
            if m < 2:
                w_in[
                    pl.ds(pl.multiple_of(p // HT * TILE, TILE), TILE),
                    pl.ds(pl.multiple_of(p % HT * TILE + m * width, TILE), TILE),
                ] = tile
            else:
                w_down[
                    pl.ds(pl.multiple_of(p // DT * TILE, TILE), TILE),
                    pl.ds(pl.multiple_of(p % DT * TILE, TILE), TILE),
                ] = tile
        return carry

    lax.fori_loop(1, half // 2 + 1, relay, 0)
    lax.fori_loop(0, LOC, place, 0)
    lax.fori_loop(half // 2 + 1, half + 1, relay, 0)

    def x_arrival(slot, carry):
        for step in range(1, nx):
            x_copy(slot, step).wait_recv()
        return carry

    lax.fori_loop(0, nz, x_arrival, 0)

    def unpack(slot, carry):
        for o in range(2):
            for xx in range(nx):
                at = pl.multiple_of(slot * 8 * per_z + xx * 16, 16)
                rows[o, pl.ds(at, 16), :] = gathered[xx, slot, o].astype(F32)
        return carry

    lax.fori_loop(0, nz, unpack, 0)
    for k in range(DT):
        tok[:, k * TILE : (k + 1) * TILE] = rows[0, pl.ds(k, tokens, stride=8), :].astype(BF16)
        cot[k] = rows[1, pl.ds(k, tokens, stride=8), :].astype(BF16)

    gate_up = jnp.dot(tok[...], w_in[...], preferred_element_type=F32)
    part[:, :, : 2 * width] = gate_up.astype(BF16).reshape(nn, own_rows, 2 * width)
    hid = jnp.zeros((tokens, width), F32)
    for k in range(DT):
        hid = hid + lax.dot_general(
            cot[k], w_down[:, k * TILE : (k + 1) * TILE],
            (((1,), (1,)), ((), ())), preferred_element_type=F32,
        )
    part[:, :, 2 * width :] = hid.astype(BF16).reshape(nn, own_rows, width)

    def p_copy(step):
        return remote(
            part.at[(me + step) % nn], part_in.at[step],
            ps.at[step], pr.at[step], at_n(step),
        )

    for step in range(1, nn):
        p_copy(step).start()

    for k in range(DT):
        tok_t[k] = rows[0, pl.ds(k, tokens, stride=8), :].T.astype(BF16)

    total = part[me].astype(F32)
    for step in range(1, nn):
        p_copy(step).wait_recv()
        total = total + part_in[step].astype(F32)
    gate_sum, up_sum = total[:, :width], total[:, width : 2 * width]
    hidden_grad = total[:, 2 * width :]
    sig = jax.nn.sigmoid(gate_sum)
    acts[me, :, :width] = (gate_sum * sig * up_sum).astype(BF16)
    acts[me, :, width : 2 * width] = (
        hidden_grad * up_sum * sig * (1.0 + gate_sum * (1.0 - sig))
    ).astype(BF16)
    acts[me, :, 2 * width :] = (hidden_grad * gate_sum * sig).astype(BF16)

    def a_copy(step):
        return remote(
            acts.at[me], acts.at[me], as_.at[step], ar.at[step], at_n(step),
        )

    for step in range(1, nn):
        a_copy(step).start()
    for step in range(1, nn):
        a_copy(step).wait_recv()

    everything = acts[...].reshape(tokens, 3 * width)
    out = jnp.dot(everything[:, :width], w_down[...], preferred_element_type=F32)
    for k in range(DT):
        rows[0, pl.ds(k, tokens, stride=8), :] = out[:, k * TILE : (k + 1) * TILE]
    both_act = everything[:, width:]
    for k in range(DT):
        rows[1, pl.ds(k, tokens, stride=8), :] = lax.dot_general(
            both_act, w_in[k * TILE : (k + 1) * TILE, :],
            (((1,), (1,)), ((), ())), preferred_element_type=F32,
        )

    def b_copy(slot, step):
        return remote(
            back.at[(x + step) % nx, slot], back_in.at[step - 1, slot],
            bs.at[step - 1, slot], br.at[step - 1, slot], at_x(step),
        )

    def far_first(q):
        d = half - (q + 1) // 2
        return jnp.where(q % 2 == 1, d, (nz - d) % nz)

    def to_x(q, carry):
        slot = far_first(q)
        for o in range(2):
            for xx in range(nx):
                at = pl.multiple_of(slot * 8 * per_z + xx * 16, 16)
                back[xx, slot, o] = rows[o, pl.ds(at, 16), :].astype(BF16)
        for step in range(1, nx):
            b_copy(slot, step).start()
        return carry

    lax.fori_loop(0, nz, to_x, 0)

    def l_copy(slot, step):
        return remote(
            back_sum.at[slot], last_in.at[(nz - slot) % nz],
            ls.at[slot], lr.at[(nz - slot) % nz], at_z(step),
        )

    def to_z(q, carry):
        slot = far_first(q)
        for step in range(1, nx):
            b_copy(slot, step).wait_recv()
        summed = back[x, slot].astype(F32)
        for step in range(1, nx):
            summed = summed + back_in[step - 1, slot].astype(F32)
        back_sum[slot] = summed.astype(BF16)

        @pl.when(q < nz - 1)
        def _():
            l_copy(slot, slot).start()

        return carry

    lax.fori_loop(0, nz, to_z, 0)

    for j in range(3 * HT):
        act[j] = everything[:, j * TILE : (j + 1) * TILE]
    for j in range(HT):
        hid_t[j] = act[j].astype(F32).T.astype(BF16)
    stores = []
    for m, to in ((0, gate_grad), (1, up_grad), (2, down_grad)):

        def tile_grad(s, carry):
            p = slots[m, 0, 0, s]
            if m < 2:
                left, right = tok_t[p // HT], act[HT * (m + 1) + p % HT]
            else:
                left, right = hid_t[p // DT], cot[p % DT]
            grad = jnp.dot(left, right, preferred_element_type=F32)
            live = (s < counts[m, 0, 0]).astype(F32)
            grads[m, s] = (grad * live).astype(BF16)
            return carry

        lax.fori_loop(0, cap, tile_grad, 0)
        store = pltpu.make_async_copy(grads.at[m], to, sem_out.at[m])
        store.start()
        stores.append(store)

    def last(slot, carry):
        l_copy((nz - slot) % nz, 0).wait_recv()
        return carry + last_in[slot].astype(F32)

    final = lax.fori_loop(1, nz, last, back_sum[0].astype(F32))
    for o, to in ((0, layer_out), (1, input_grad)):
        pair[o] = final[o]
        for k in range(DT):
            for i in range(2):
                to[i : i + 1, k * TILE : (k + 1) * TILE] = pair[
                    o, pl.ds(8 * i + k, 1), :
                ].astype(BF16)

    def sent_x(slot, carry):
        for step in range(1, nx):
            x_copy(slot, step).wait_send()
            b_copy(slot, step).wait_send()
        return carry

    lax.fori_loop(0, nz, sent_x, 0)

    def sent_z(slot, carry):
        z_copy(slot, slot, 0).wait_send()
        l_copy(slot, 0).wait_send()
        return carry

    lax.fori_loop(1, nz, sent_z, 0)
    for step in range(1, nn):
        p_copy(step).wait_send()
        a_copy(step).wait_send()
    for store in stores:
        store.wait()


def per_device(nz, nx, nn, tokens, cotangent, gate_tiles, up_tiles, down_tiles, slots, counts):
    cap = gate_tiles.shape[2]
    count = 2 * nz * nx
    own = count // nn
    block = (cap, TILE, TILE)
    width = HT * TILE
    features = DT * TILE
    dma = pltpu.SemaphoreType.DMA
    vmem = pltpu.VMEM
    anywhere = pl.BlockSpec(memory_space=pl.ANY)
    smem = pl.BlockSpec(memory_space=pltpu.SMEM)
    in_vmem = pl.BlockSpec(memory_space=pltpu.VMEM)
    results = pl.pallas_call(
        functools.partial(layer_kernel, nz, nx, nn, cap),
        out_shape=(
            jax.ShapeDtypeStruct(tokens.shape, BF16),
            jax.ShapeDtypeStruct(tokens.shape, BF16),
            jax.ShapeDtypeStruct(block, BF16),
            jax.ShapeDtypeStruct(block, BF16),
            jax.ShapeDtypeStruct(block, BF16),
        ),
        in_specs=[smem, smem] + [anywhere] * 5,
        out_specs=(in_vmem, in_vmem, anywhere, anywhere, anywhere),
        scratch_shapes=[
            vmem((2, 2, features), BF16),
            vmem((2, 16, TILE), F32),
            vmem((nx, nz, 2, 16, TILE), BF16),
            vmem((3, *block), BF16),
            vmem((features, 2 * width), BF16),
            vmem((width, features), BF16),
            vmem((2, count * 8, TILE), F32),
            vmem((count, features), BF16),
            vmem((DT, count, TILE), BF16),
            vmem((DT, TILE, count), BF16),
            vmem((HT, TILE, count), BF16),
            vmem((3 * HT, count, TILE), BF16),
            vmem((nn, own, 3 * width), BF16),
            vmem((nn, own, 3 * width), BF16),
            vmem((nn, own, 3 * width), BF16),
            vmem((nx, nz, 2, 16, TILE), BF16),
            vmem((nx - 1, nz, 2, 16, TILE), BF16),
            vmem((nz, 2, 16, TILE), BF16),
            vmem((nz, 2, 16, TILE), BF16),
            vmem((3, *block), BF16),
            dma((5,)),
            dma((3,)),
            dma((nz,)),
            dma((nz,)),
            dma((nx - 1, nz)),
            dma((nx - 1, nz)),
            dma((nn,)),
            dma((nn,)),
            dma((nn,)),
            dma((nn,)),
            dma((nx - 1, nz)),
            dma((nx - 1, nz)),
            dma((nz,)),
            dma((nz,)),
        ],
        compiler_params=pltpu.CompilerParams(collective_id=0, has_side_effects=True),
        name="pruned_layer",
    )(
        slots, counts, tokens, cotangent,
        gate_tiles.reshape(block), up_tiles.reshape(block), down_tiles.reshape(block),
    )
    layer_out, input_grad, *tile_grads = results
    return (layer_out, input_grad, *(g[None, None] for g in tile_grads))


def solution(mesh, x_size=X_SIZE):
    tiles = P("narrow", "wide", None, None, None)
    panel = P("wide", "narrow")
    wide, narrow = mesh.shape["wide"], mesh.shape["narrow"]
    return jax.shard_map(
        functools.partial(per_device, wide // x_size, x_size, narrow),
        mesh=mesh,
        in_specs=(
            panel, panel, tiles, tiles, tiles,
            P(None, "narrow", "wide", None), P(None, "narrow", "wide"),
        ),
        out_specs=(panel, panel, tiles, tiles, tiles),
        check_vma=False,
    )
```

time: 223 us -> 69.6 us (0.31)
  the two profiles are of different devices: /device:TPU:24 before, /device:TPU:1 now
where the time goes in v1:
time: 69.6 us; the launch traced here: 69.3 us
  Pallas kernels  61.7 us (89%)
  local copies, waits for them, and re-layouts  6.94 us (10%)
    pallas_call x1, Pallas kernels, per_device(): pl.pallas_call(functools.partial(layer_kernel, nz, nx, nn, cap), out_shap...  61.7 us
    unnamed x16, local copies, waits for them, and re-layouts  6.94 us

profile of v1, /device:TPU:1, one launch (start us, length us, event | category | flops | bytes accessed | tf_op | source)
XLA Modules:
  0.0 69.3 jit_solution(6850145879338129717)
XLA Ops:
  0.6 0.0 copy-start.4
  0.6 0.6 copy-done.4
  1.3 0.6 copy.12.counts
  1.9 61.7 %pruned_layer.1 = (bf16[2,1024]{1,0:T(2,128)(2,1)}, bf16[2,1024]{1,0:T(2,128)(2,1)}, bf16[12,128,128]{2,1,0:T(8,128)(2,1)}, bf16[12,128,128]{2,1,0:T(8,128)(2,1)}, bf16[12,128,128]{2,1,0:T(8,128)(2,1)}) custom-call(s32[3,1,1,12]{3,2,1,0:T(1,128)} %slots.1, s32[3,1,1]{2,1,0:T(1,128)} %copy.12.counts, bf16[2,1024]{1,0:T(2,128)(2,1)} %tok_hbm.1, ...), custom_call_target="tpu_custom_call" | custom-call | tf_op jit(solution)/shard_map/pruned_layer/pallas_call | solution.py:340
  63.6 0.0 copy-start.3
  63.6 0.7 copy-done.3
  64.3 0.0 copy-start.2
  64.3 0.6 copy.18
  64.9 0.1 copy-done.2
  65.0 0.6 copy.19
  65.6 0.0 copy-start.1
  65.6 1.8 %copy.20 = bf16[1,1,12,128,128]{4,3,2,1,0:T(8,128)(2,1)} copy(bf16[1,1,12,128,128]{4,3,2,1,0:T(8,128)(2,1)} %bitcast.8) | data formatting | bytes 786432
  67.4 0.0 copy-done.1
  67.4 0.0 copy-start
  67.4 0.7 %copy.21 = bf16[1,1,12,128,128]{4,3,2,1,0:T(8,128)(2,1)} copy(bf16[1,1,12,128,128]{4,3,2,1,0:T(8,128)(2,1)S(1)} %bitcast.7) | data formatting | bytes 786432
  68.1 0.4 copy-done
  68.5 0.7 %copy.22 = bf16[1,1,12,128,128]{4,3,2,1,0:T(8,128)(2,1)} copy(bf16[1,1,12,128,128]{4,3,2,1,0:T(8,128)(2,1)S(1)} %bitcast.6) | data formatting | bytes 786432
Async XLA Ops:
  0.6 0.7 copy-start.4
  63.6 0.7 copy-start.3
  64.3 0.7 copy-start.2
  65.6 1.8 %copy-start.1 = (bf16[12,128,128]{2,1,0:T(8,128)(2,1)S(1)}, bf16[12,128,128]{2,1,0:T(8,128)(2,1)}, u32[]{:S(2)}) copy-start(bf16[12,128,128]{2,1,0:T(8,128)(2,1)} %get-tuple-element.13) | copy-start | bytes 1179652
  67.4 1.1 %copy-start = (bf16[12,128,128]{2,1,0:T(8,128)(2,1)S(1)}, bf16[12,128,128]{2,1,0:T(8,128)(2,1)}, u32[]{:S(2)}) copy-start(bf16[12,128,128]{2,1,0:T(8,128)(2,1)} %get-tuple-element.14) | copy-start | bytes 1179652

commit v2 on v1

v2 whole, which is shorter than its diff:
```python
import functools

import jax
import jax.numpy as jnp
from jax import lax
from jax.experimental import pallas as pl
from jax.experimental.pallas import tpu as pltpu
from jax.sharding import PartitionSpec as P

TILE = 128
HT = 3
DT = 8
LOC = HT * DT
X_SIZE = 4
VMEM_LIMIT = 24 * 1024 * 1024
F32, BF16 = jnp.float32, jnp.bfloat16
MESH = pl.DeviceIdType.MESH


def layer_kernel(
    nz, nx, nn, cap,
    slots_hbm, counts_hbm, tok_hbm, cot_hbm, gate_hbm, up_hbm, down_hbm,
    layer_out, input_grad, grads,
    slots, counts, own_in, pair, gathered, tiles, keys, w_in, w_down, rows, rows_out,
    tok, cot, tok_t, hid_t, act,
    part_own, part, part_in, acts, back, back_in, back_sum, last_in,
    sem_in, zs, zr, xs, xr, ps, pr, as_, ar, bs, br, ls, lr,
):
    wide, me = lax.axis_index("wide"), lax.axis_index("narrow")
    z, x = wide // nx, wide % nx
    half, reach = nz // 2, nz // 4
    width = HT * TILE
    features = DT * TILE
    tokens = 2 * nz * nx
    per_z = 2 * nx
    in_chunk = tokens // 2
    own_rows = in_chunk // nn
    home = reach - 1

    def at_z(step):
        return ((z + step + nz) % nz * nx + x, me)

    def at_x(step):
        return (z * nx + (x + step) % nx, me)

    def at_n(step):
        return (wide, (me + step) % nn)

    def slot_of(step):
        return (home + step + nz) % nz

    def remote(src, dst, send, recv, target):
        return pltpu.make_async_remote_copy(
            src_ref=src, dst_ref=dst, send_sem=send, recv_sem=recv,
            device_id=target, device_id_type=MESH,
        )

    barrier = pltpu.get_barrier_semaphore()
    z_near = sorted({s % nz for d in range(1, reach + 1) for s in (d, -d)})
    for step in z_near:
        pl.semaphore_signal(barrier, inc=1, device_id=at_z(step), device_id_type=MESH)
    for step in range(1, nx):
        pl.semaphore_signal(barrier, inc=1, device_id=at_x(step), device_id_type=MESH)
    for step in range(1, nn):
        pl.semaphore_signal(barrier, inc=1, device_id=at_n(step), device_id_type=MESH)

    loads = [
        pltpu.make_async_copy(tok_hbm, own_in.at[0], sem_in.at[0]),
        pltpu.make_async_copy(cot_hbm, own_in.at[1], sem_in.at[1]),
        pltpu.make_async_copy(gate_hbm, tiles.at[0], sem_in.at[2]),
        pltpu.make_async_copy(up_hbm, tiles.at[1], sem_in.at[3]),
        pltpu.make_async_copy(down_hbm, tiles.at[2], sem_in.at[4]),
        pltpu.make_async_copy(slots_hbm, slots, sem_in.at[5]),
        pltpu.make_async_copy(counts_hbm, counts, sem_in.at[6]),
    ]
    for load in loads:
        load.start()

    loads[0].wait()
    loads[1].wait()
    for o in range(2):
        both = own_in[o].astype(F32)
        for k in range(DT):
            for i in range(2):
                pair[o, pl.ds(8 * i + k, 1), :] = both[i : i + 1, k * TILE : (k + 1) * TILE]
        gathered[x, home, o] = pair[o].astype(BF16)

    pl.semaphore_wait(barrier, len(z_near) + nx - 1 + nn - 1)

    def z_copy(slot, step):
        to_slot = (slot - step + nz) % nz
        return remote(
            gathered.at[x, slot], gathered.at[x, to_slot],
            zs.at[to_slot], zr.at[to_slot], at_z(step),
        )

    def z_arrival(slot):
        return remote(
            gathered.at[x, slot], gathered.at[x, slot], zs.at[slot], zr.at[slot], at_z(1),
        )

    def x_copy(slot, step):
        return remote(
            gathered.at[x, slot], gathered.at[x, slot],
            xs.at[step - 1, slot], xr.at[step - 1, slot], at_x(step),
        )

    for d in range(1, reach + 1):
        z_copy(home, d).start()
        z_copy(home, -d).start()
    for step in range(1, nx):
        x_copy(home, step).start()

    def relay(d, carry):
        behind = slot_of(-d)
        z_arrival(behind).wait_recv()

        @pl.when(d + reach <= half)
        def _():
            z_copy(behind, reach).start()

        @pl.when(d < half)
        def _():
            ahead = slot_of(d)
            z_arrival(ahead).wait_recv()

            @pl.when(d + reach < half)
            def _():
                z_copy(ahead, -reach).start()

            for step in range(1, nx):
                x_copy(ahead, step).start()

        for step in range(1, nx):
            x_copy(behind, step).start()
        return carry

    for load in loads[2:]:
        load.wait()
    for m in range(3):
        for s in range(cap):
            keys[m, s] = jnp.where(s < counts[0, 0, m], slots[m, 0, 0, s], -1)

    def place(m, p, carry):
        found = jnp.int32(-1)
        for s in range(cap):
            found = jnp.where(keys[m, s] == p, s, found)
        live = found >= 0
        tile = tiles[m, jnp.where(live, found, 0)]
        tile = jnp.where(live, tile, jnp.zeros_like(tile))
        if m < 2:
            w_in[
                pl.ds(pl.multiple_of(p // HT * TILE, TILE), TILE),
                pl.ds(pl.multiple_of(p % HT * TILE + m * width, TILE), TILE),
            ] = tile
        else:
            w_down[
                pl.ds(pl.multiple_of(p // DT * TILE, TILE), TILE),
                pl.ds(pl.multiple_of(p % DT * TILE, TILE), TILE),
            ] = tile
        return carry

    def unpack(c):
        def one(slot, carry):
            for step in range(1, nx):
                x_copy(slot, step).wait_recv()
            for o in range(2):
                for xx in range(nx):
                    at = pl.multiple_of(slot * 8 * per_z + xx * 16, 16)
                    rows[o, pl.ds(at, 16), :] = gathered[xx, slot, o].astype(F32)
            return carry

        lax.fori_loop(c * half, (c + 1) * half, one, 0)
        here = pl.ds(c * in_chunk, in_chunk)
        for k in range(DT):
            picked = pl.ds(c * in_chunk * 8 + k, in_chunk, stride=8)
            tok[here, k * TILE : (k + 1) * TILE] = rows[0, picked, :].astype(BF16)
            cot[k, here, :] = rows[1, picked, :].astype(BF16)

    def p_copy(c, step):
        return remote(
            part.at[c, (me + step) % nn], part_in.at[c, step],
            ps.at[c, step], pr.at[c, step], at_n(step),
        )

    def front(c):
        here = pl.ds(c * in_chunk, in_chunk)
        gate_up = jnp.dot(tok[here, :], w_in[...], preferred_element_type=F32)
        hid = jnp.zeros((in_chunk, width), F32)
        for k in range(DT):
            hid = hid + lax.dot_general(
                cot[k, here, :], w_down[:, k * TILE : (k + 1) * TILE],
                (((1,), (1,)), ((), ())), preferred_element_type=F32,
            )
        for value, at in ((gate_up, 0), (hid, 2 * width)):
            value = value.reshape(nn, own_rows, value.shape[1])
            part_own[c, :, :, at : at + value.shape[2]] = value
            part[c, :, :, at : at + value.shape[2]] = value.astype(BF16)
        for step in range(1, nn):
            p_copy(c, step).start()

    def a_copy(c, step):
        return remote(
            acts.at[c, me], acts.at[c, me], as_.at[c, step], ar.at[c, step], at_n(step),
        )

    def middle(c):
        total = part_own[c, me]
        for step in range(1, nn):
            p_copy(c, step).wait_recv()
            total = total + part_in[c, step].astype(F32)
        gate_sum, up_sum = total[:, :width], total[:, width : 2 * width]
        hidden_grad = total[:, 2 * width :]
        sig = jax.nn.sigmoid(gate_sum)
        acts[c, me, :, :width] = (gate_sum * sig * up_sum).astype(BF16)
        acts[c, me, :, width : 2 * width] = (
            hidden_grad * up_sum * sig * (1.0 + gate_sum * (1.0 - sig))
        ).astype(BF16)
        acts[c, me, :, 2 * width :] = (hidden_grad * gate_sum * sig).astype(BF16)
        for step in range(1, nn):
            a_copy(c, step).start()

    def b_copy(slot, step):
        return remote(
            back.at[(x + step) % nx, slot], back_in.at[step - 1, slot],
            bs.at[step - 1, slot], br.at[step - 1, slot], at_x(step),
        )

    def far_first(c, q):
        d = half - c_start(c) - (q + 1) // 2
        return slot_of(jnp.where(q % 2 == 0, d, nz - d))

    def c_start(c):
        return 0 if c else reach

    def finish(c):
        here = pl.ds(c * in_chunk, in_chunk)
        for step in range(1, nn):
            a_copy(c, step).wait_recv()
        everything = acts[c].astype(F32).reshape(in_chunk, 3 * width).astype(BF16)
        for j in range(3 * HT):
            act[j, here, :] = everything[:, j * TILE : (j + 1) * TILE]
        out = jnp.dot(everything[:, :width], w_down[...], preferred_element_type=F32)
        both_act = everything[:, width:]
        for k in range(DT):
            picked = pl.ds(c * in_chunk * 8 + k, in_chunk, stride=8)
            rows_out[0, picked, :] = out[:, k * TILE : (k + 1) * TILE]
            rows_out[1, picked, :] = lax.dot_general(
                both_act, w_in[k * TILE : (k + 1) * TILE, :],
                (((1,), (1,)), ((), ())), preferred_element_type=F32,
            )

        def to_x(q, carry):
            slot = far_first(c, q)
            for o in range(2):
                for xx in range(nx):
                    at = pl.multiple_of(slot * 8 * per_z + xx * 16, 16)
                    back[xx, slot, o] = rows_out[o, pl.ds(at, 16), :].astype(BF16)
            for step in range(1, nx):
                b_copy(slot, step).start()
            return carry

        lax.fori_loop(0, half, to_x, 0)

    def l_copy(slot):
        step = slot - home
        to_slot = slot_of(-step)
        return remote(
            back_sum.at[slot], last_in.at[to_slot], ls.at[slot], lr.at[to_slot], at_z(step),
        )

    def l_arrival(slot):
        return remote(
            back_sum.at[slot], last_in.at[slot], ls.at[slot], lr.at[slot], at_z(1),
        )

    def summed_over_x(slot):
        for step in range(1, nx):
            b_copy(slot, step).wait_recv()
        at = pl.multiple_of(slot * 8 * per_z + x * 16, 16)
        total = rows_out[:, pl.ds(at, 16), :]
        for step in range(1, nx):
            total = total + back_in[step - 1, slot].astype(F32)
        return total

    def to_z(c):
        def one(q, carry):
            slot = far_first(c, q)
            back_sum[slot] = summed_over_x(slot).astype(BF16)
            l_copy(slot).start()
            return carry

        lax.fori_loop(0, half if c else half - 1, one, 0)

    split = reach + (half - reach) // 2
    lax.fori_loop(0, LOC // 2, functools.partial(place, 0), 0)
    lax.fori_loop(1, reach + 1, relay, 0)
    lax.fori_loop(LOC // 2, LOC, functools.partial(place, 0), 0)
    lax.fori_loop(0, LOC, functools.partial(place, 1), 0)
    lax.fori_loop(0, LOC, functools.partial(place, 2), 0)
    lax.fori_loop(reach + 1, split + 1, relay, 0)
    unpack(0)
    front(0)
    lax.fori_loop(split + 1, half + 1, relay, 0)
    middle(0)
    unpack(1)
    front(1)
    finish(0)
    middle(1)
    to_z(0)
    for k in range(DT):
        tok_t[k] = rows[0, pl.ds(k, tokens, stride=8), :].T.astype(BF16)
    finish(1)
    to_z(1)

    for j in range(HT):
        hid_t[j] = act[j].astype(F32).T.astype(BF16)
    for m in range(3):

        def tile_grad(s, carry):
            p = slots[m, 0, 0, s]
            if m < 2:
                left, right = tok_t[p // HT], act[HT * (m + 1) + p % HT]
            else:
                left, right = hid_t[p // DT], cot[p % DT]
            grad = jnp.dot(left, right, preferred_element_type=F32)
            live = (s < counts[0, 0, m]).astype(F32)
            grads[m, s] = (grad * live).astype(BF16)
            return carry

        lax.fori_loop(0, cap, tile_grad, 0, unroll=4)

    def last(slot, carry):
        l_arrival(slot).wait_recv()
        return carry + last_in[slot].astype(F32)

    final = lax.fori_loop(0, home, last, summed_over_x(home))
    final = lax.fori_loop(home + 1, nz, last, final)
    for o, to in ((0, layer_out), (1, input_grad)):
        pair[o] = final[o]
        for k in range(DT):
            for i in range(2):
                to[i : i + 1, k * TILE : (k + 1) * TILE] = pair[
                    o, pl.ds(8 * i + k, 1), :
                ].astype(BF16)

    def sent(slot, carry):
        for step in range(1, nx):
            x_copy(slot, step).wait_send()
            b_copy(slot, step).wait_send()

        @pl.when(slot != home)
        def _():
            z_arrival(slot).wait_send()
            l_copy(slot).wait_send()

        return carry

    lax.fori_loop(0, nz, sent, 0)
    for c in range(2):
        for step in range(1, nn):
            p_copy(c, step).wait_send()
            a_copy(c, step).wait_send()


def write_kernel(*refs):
    sems = refs[-1]
    layer_out, input_grad, grads, *outs = refs[:-1]
    sources = (layer_out, input_grad, grads.at[0], grads.at[1], grads.at[2])
    stores = [
        pltpu.make_async_copy(source, to, sems.at[i])
        for i, (source, to) in enumerate(zip(sources, outs))
    ]
    for store in stores:
        store.start()
    for store in stores:
        store.wait()


def per_device(nz, nx, nn, tokens, cotangent, gate_tiles, up_tiles, down_tiles, slots, counts):
    cap = gate_tiles.shape[2]
    count = 2 * nz * nx
    own = count // 2 // nn
    block = (cap, TILE, TILE)
    width = HT * TILE
    features = DT * TILE
    dma = pltpu.SemaphoreType.DMA
    vmem = pltpu.VMEM
    anywhere = pl.BlockSpec(memory_space=pl.ANY)
    in_hbm = pl.BlockSpec(memory_space=pltpu.HBM)
    in_vmem = pl.BlockSpec(memory_space=pltpu.VMEM)
    results = pl.pallas_call(
        functools.partial(layer_kernel, nz, nx, nn, cap),
        out_shape=(
            vmem(tokens.shape, BF16),
            vmem(tokens.shape, BF16),
            vmem((3, *block), BF16),
        ),
        in_specs=[in_hbm] * 7,
        out_specs=(in_vmem, in_vmem, in_vmem),
        scratch_shapes=[
            pltpu.SMEM(slots.shape, jnp.int32),
            pltpu.SMEM((1, 1, 3), jnp.int32),
            vmem((2, 2, features), BF16),
            vmem((2, 16, TILE), F32),
            vmem((nx, nz, 2, 16, TILE), BF16),
            vmem((3, *block), BF16),
            pltpu.SMEM((3, cap), jnp.int32),
            vmem((features, 2 * width), BF16),
            vmem((width, features), BF16),
            vmem((2, count * 8, TILE), F32),
            vmem((2, count * 8, TILE), F32),
            vmem((count, features), BF16),
            vmem((DT, count, TILE), BF16),
            vmem((DT, TILE, count), BF16),
            vmem((HT, TILE, count), BF16),
            vmem((3 * HT, count, TILE), BF16),
            vmem((2, nn, own, 3 * width), F32),
            vmem((2, nn, own, 3 * width), BF16),
            vmem((2, nn, own, 3 * width), BF16),
            vmem((2, nn, own, 3 * width), BF16),
            vmem((nx, nz, 2, 16, TILE), BF16),
            vmem((nx - 1, nz, 2, 16, TILE), BF16),
            vmem((nz, 2, 16, TILE), BF16),
            vmem((nz, 2, 16, TILE), BF16),
            dma((7,)),
            dma((nz,)),
            dma((nz,)),
            dma((nx - 1, nz)),
            dma((nx - 1, nz)),
            dma((2, nn)),
            dma((2, nn)),
            dma((2, nn)),
            dma((2, nn)),
            dma((nx - 1, nz)),
            dma((nx - 1, nz)),
            dma((nz,)),
            dma((nz,)),
        ],
        compiler_params=pltpu.CompilerParams(
            collective_id=0, has_side_effects=True, vmem_limit_bytes=VMEM_LIMIT
        ),
        name="pruned_layer",
    )(
        *[
            pltpu.with_memory_space_constraint(a, pltpu.HBM)
            for a in (
                slots, jnp.transpose(counts, (1, 2, 0)), tokens, cotangent,
                gate_tiles.reshape(block), up_tiles.reshape(block), down_tiles.reshape(block),
            )
        ]
    )
    layer_out, input_grad, *tile_grads = pl.pallas_call(
        write_kernel,
        out_shape=(
            jax.ShapeDtypeStruct(tokens.shape, BF16),
            jax.ShapeDtypeStruct(tokens.shape, BF16),
            *[jax.ShapeDtypeStruct(block, BF16)] * 3,
        ),
        in_specs=[in_vmem] * 3,
        out_specs=(anywhere,) * 5,
        scratch_shapes=[dma((5,))],
        compiler_params=pltpu.CompilerParams(vmem_limit_bytes=VMEM_LIMIT),
        name="write",
    )(*results)
    return (layer_out, input_grad, *(g[None, None] for g in tile_grads))


def solution(mesh, x_size=X_SIZE):
    tiles = P("narrow", "wide", None, None, None)
    panel = P("wide", "narrow")
    wide, narrow = mesh.shape["wide"], mesh.shape["narrow"]
    return jax.shard_map(
        functools.partial(per_device, wide // x_size, x_size, narrow),
        mesh=mesh,
        in_specs=(
            panel, panel, tiles, tiles, tiles,
            P(None, "narrow", "wide", None), P(None, "narrow", "wide"),
        ),
        out_specs=(panel, panel, tiles, tiles, tiles),
        check_vma=False,
    )
```

time: 69.6 us -> 55.9 us (0.80)
  the two profiles are of different devices: /device:TPU:1 before, /device:TPU:24 now
where the time goes in v2:
time: 55.9 us; the launch traced here: 55.8 us
  Pallas kernels  55.2 us (99%)
  between operations  0.64 us (1%)
    pallas_call x1, Pallas kernels, per_device(): pl.pallas_call(functools.partial(layer_kernel, nz, nx, nn, cap), out_shap...  54.1 us

profile of v2, /device:TPU:24, one launch (start us, length us, event | category | flops | bytes accessed | tf_op | source)
XLA Modules:
  0.0 55.8 jit_solution(10653892545928691315)
XLA Ops:
  0.6 54.1 %pruned_layer.1 = (bf16[2,1024]{1,0:T(2,128)(2,1)S(1)}, bf16[2,1024]{1,0:T(2,128)(2,1)S(1)}, bf16[3,12,128,128]{3,2,1,0:T(8,128)(2,1)S(1)}) custom-call(s32[3,1,1,12]{3,2,1,0:T(1,128)} %slots_hbm.1, s32[1,1,3]{2,1,0:T(1,128)} %bitcast.10, bf16[2,1024]{1,0:T(2,128)(2,1)} %tok_hbm.1, bf16[2,1024]{1,0:T(2,128)(2,1)} %cot_hbm.1, bf16[12,128,128]{2,1,0:T(8,128)(2,1)} %bitcast.7, ...), custom_call_target="tpu_custom_call" | custom-call | tf_op jit(solution)/shard_map/pruned_layer/pallas_call | solution.py:392
  54.7 1.1 %write.1 = (bf16[2,1024]{1,0:T(2,128)(2,1)}, bf16[2,1024]{1,0:T(2,128)(2,1)}, bf16[12,128,128]{2,1,0:T(8,128)(2,1)}, bf16[12,128,128]{2,1,0:T(8,128)(2,1)}, bf16[12,128,128]{2,1,0:T(8,128)(2,1)}) custom-call(bf16[2,1024]{1,0:T(2,128)(2,1)S(1)} %get-tuple-element.13.refs_0_, bf16[2,1024]{1,0:T(2,128)(2,1)S(1)} %get-tuple-element.14.refs_1_, ...), custom_call_target="tpu_custom_call" | custom-call | tf_op jit(solution)/shard_map/write/pallas_call | solution.py:453

commit v3 on v2

--- a/solution.py
+++ b/solution.py
@@ -15,6 +15,10 @@
 VMEM_LIMIT = 24 * 1024 * 1024
 F32, BF16 = jnp.float32, jnp.bfloat16
 MESH = pl.DeviceIdType.MESH
+
+
+def far_order(ring):
+    return sorted(range(1, ring), key=lambda step: -min(step, ring - step))
 
 
 def layer_kernel(
@@ -108,7 +112,7 @@
     for d in range(1, reach + 1):
         z_copy(home, d).start()
         z_copy(home, -d).start()
-    for step in range(1, nx):
+    for step in far_order(nx):
         x_copy(home, step).start()
 
     def relay(d, carry):
@@ -128,10 +132,10 @@
             def _():
                 z_copy(ahead, -reach).start()
 
-            for step in range(1, nx):
+            for step in far_order(nx):
                 x_copy(ahead, step).start()
 
-        for step in range(1, nx):
+        for step in far_order(nx):
             x_copy(behind, step).start()
         return carry
 
@@ -196,7 +200,7 @@
             value = value.reshape(nn, own_rows, value.shape[1])
             part_own[c, :, :, at : at + value.shape[2]] = value
             part[c, :, :, at : at + value.shape[2]] = value.astype(BF16)
-        for step in range(1, nn):
+        for step in far_order(nn):
             p_copy(c, step).start()
 
     def a_copy(c, step):
@@ -217,7 +221,7 @@
             hidden_grad * up_sum * sig * (1.0 + gate_sum * (1.0 - sig))
         ).astype(BF16)
         acts[c, me, :, 2 * width :] = (hidden_grad * gate_sum * sig).astype(BF16)
-        for step in range(1, nn):
+        for step in far_order(nn):
             a_copy(c, step).start()
 
     def b_copy(slot, step):
@@ -256,7 +260,7 @@
                 for xx in range(nx):
                     at = pl.multiple_of(slot * 8 * per_z + xx * 16, 16)
                     back[xx, slot, o] = rows_out[o, pl.ds(at, 16), :].astype(BF16)
-            for step in range(1, nx):
+            for step in far_order(nx):
                 b_copy(slot, step).start()
             return carry
 
@@ -302,16 +306,16 @@
     unpack(0)
     front(0)
     lax.fori_loop(split + 1, half + 1, relay, 0)
-    middle(0)
     unpack(1)
     front(1)
+    middle(0)
+    middle(1)
     finish(0)
-    middle(1)
+    finish(1)
     to_z(0)
+    to_z(1)
     for k in range(DT):
         tok_t[k] = rows[0, pl.ds(k, tokens, stride=8), :].T.astype(BF16)
-    finish(1)
-    to_z(1)
 
     for j in range(HT):
         hid_t[j] = act[j].astype(F32).T.astype(BF16)

time: 55.9 us -> 53.4 us (0.955)
  Pallas kernels: 55.2 us -> 52.6 us
    pallas_call x1, Pallas kernels: 54.1 us -> 51.5 us  [per_device(): pl.pallas_call(functools.partial(layer_kernel, nz, nx, nn, cap), out_shap...]
where the time goes in v3:
time: 53.4 us; the launch traced here: 53.2 us
  Pallas kernels  52.6 us (99%)
  between operations  0.64 us (1%)
    pallas_call x1, Pallas kernels, per_device(): pl.pallas_call(functools.partial(layer_kernel, nz, nx, nn, cap), out_shap...  51.5 us

profile of v3, /device:TPU:24, one launch (start us, length us, event | category | flops | bytes accessed | tf_op | source)
XLA Modules:
  0.0 53.2 jit_solution(8947729092909566479)
XLA Ops:
  0.6 51.5 %pruned_layer.1 = (bf16[2,1024]{1,0:T(2,128)(2,1)S(1)}, bf16[2,1024]{1,0:T(2,128)(2,1)S(1)}, bf16[3,12,128,128]{3,2,1,0:T(8,128)(2,1)S(1)}) custom-call(s32[3,1,1,12]{3,2,1,0:T(1,128)} %slots_hbm.1, s32[1,1,3]{2,1,0:T(1,128)} %bitcast.10, bf16[2,1024]{1,0:T(2,128)(2,1)} %tok_hbm.1, bf16[2,1024]{1,0:T(2,128)(2,1)} %cot_hbm.1, bf16[12,128,128]{2,1,0:T(8,128)(2,1)} %bitcast.7, ...), custom_call_target="tpu_custom_call" | custom-call | tf_op jit(solution)/shard_map/pruned_layer/pallas_call | solution.py:396
  52.2 1.1 %write.1 = (bf16[2,1024]{1,0:T(2,128)(2,1)}, bf16[2,1024]{1,0:T(2,128)(2,1)}, bf16[12,128,128]{2,1,0:T(8,128)(2,1)}, bf16[12,128,128]{2,1,0:T(8,128)(2,1)}, bf16[12,128,128]{2,1,0:T(8,128)(2,1)}) custom-call(bf16[2,1024]{1,0:T(2,128)(2,1)S(1)} %get-tuple-element.13.refs_0_, bf16[2,1024]{1,0:T(2,128)(2,1)S(1)} %get-tuple-element.14.refs_1_, ...), custom_call_target="tpu_custom_call" | custom-call | tf_op jit(solution)/shard_map/write/pallas_call | solution.py:457

commit v4 on v3

--- a/solution.py
+++ b/solution.py
@@ -109,7 +109,7 @@
             xs.at[step - 1, slot], xr.at[step - 1, slot], at_x(step),
         )
 
-    for d in range(1, reach + 1):
+    for d in range(reach, 0, -1):
         z_copy(home, d).start()
         z_copy(home, -d).start()
     for step in far_order(nx):

time: 53.4 us -> 53 us (level)
  Pallas kernels: 52.6 us -> 51.8 us
    pallas_call x1, Pallas kernels: 51.5 us -> 50.7 us  [per_device(): pl.pallas_call(functools.partial(layer_kernel, nz, nx, nn, cap), out_shap...]
where the time goes in v4:
time: 53 us; the launch traced here: 52.4 us
  Pallas kernels  51.8 us (98%)
  between operations  0.64 us (1%)
    pallas_call x1, Pallas kernels, per_device(): pl.pallas_call(functools.partial(layer_kernel, nz, nx, nn, cap), out_shap...  50.7 us

profile of v4, /device:TPU:24, one launch (start us, length us, event | category | flops | bytes accessed | tf_op | source)
XLA Modules:
  0.0 52.4 jit_solution(3354587656513937654)
XLA Ops:
  0.6 50.7 %pruned_layer.1 = (bf16[2,1024]{1,0:T(2,128)(2,1)S(1)}, bf16[2,1024]{1,0:T(2,128)(2,1)S(1)}, bf16[3,12,128,128]{3,2,1,0:T(8,128)(2,1)S(1)}) custom-call(s32[3,1,1,12]{3,2,1,0:T(1,128)} %slots_hbm.1, s32[1,1,3]{2,1,0:T(1,128)} %bitcast.10, bf16[2,1024]{1,0:T(2,128)(2,1)} %tok_hbm.1, bf16[2,1024]{1,0:T(2,128)(2,1)} %cot_hbm.1, bf16[12,128,128]{2,1,0:T(8,128)(2,1)} %bitcast.7, ...), custom_call_target="tpu_custom_call" | custom-call | tf_op jit(solution)/shard_map/pruned_layer/pallas_call | solution.py:396
  51.4 1.1 %write.1 = (bf16[2,1024]{1,0:T(2,128)(2,1)}, bf16[2,1024]{1,0:T(2,128)(2,1)}, bf16[12,128,128]{2,1,0:T(8,128)(2,1)}, bf16[12,128,128]{2,1,0:T(8,128)(2,1)}, bf16[12,128,128]{2,1,0:T(8,128)(2,1)}) custom-call(bf16[2,1024]{1,0:T(2,128)(2,1)S(1)} %get-tuple-element.13.refs_0_, bf16[2,1024]{1,0:T(2,128)(2,1)S(1)} %get-tuple-element.14.refs_1_, ...), custom_call_target="tpu_custom_call" | custom-call | tf_op jit(solution)/shard_map/write/pallas_call | solution.py:457
